TPU v7x, 32 devices: a whole 2x2x4 slice. The times are simulated.
32 devices in a mesh: rep: 4 (over x, core), shard: 8 (over z, y).
Axes of the slice: x: 2, y: 2, z: 4, core: 2. Of those that a mesh axis runs over, the one named last changes fastest.
Arguments:
- tokens: bfloat16 [4096, 768], P(('rep', 'shard')), may hold values from -6 to 6
- segment_ids: int32 [4096], P(('rep', 'shard')), may hold values from 0 to 3, as said below
- cotangent: bfloat16 [4096, 768], P(('rep', 'shard')), may hold values from -6 to 6
- ln1_gain: bfloat16 [1, 768], P(None, 'shard'), may hold values from 0.25 to 1.75
- ln1_bias: bfloat16 [1, 768], P(None, 'shard'), may hold values from -3 to 3
- qkv_weight: bfloat16 [1, 768, 2304], P(None, 'shard'), may hold values from -0.21875 to 0.21875
- qv_bias: bfloat16 [1, 1536], P(None, 'shard'), may hold values from -3 to 3
- out_weight: bfloat16 [1, 768, 768], P(None, 'shard'), may hold values from -0.875 to 0.875
- out_bias: bfloat16 [1, 768], P(None, 'shard'), may hold values from -3 to 3
- ln2_gain: bfloat16 [1, 768], P(None, 'shard'), may hold values from 0.25 to 1.75
- ln2_bias: bfloat16 [1, 768], P(None, 'shard'), may hold values from -3 to 3
- fc_weight: bfloat16 [1, 768, 3072], P(None, 'shard'), may hold values from -0.21875 to 0.21875
- fc_bias: bfloat16 [1, 3072], P(None, 'shard'), may hold values from -3 to 3
- proj_weight: bfloat16 [1, 3072, 768], P(None, 'shard'), may hold values from -0.109375 to 0.109375
- proj_bias: bfloat16 [1, 768], P(None, 'shard'), may hold values from -3 to 3
Outputs:
- out_tokens: bfloat16 [4096, 768], P(('rep', 'shard'))
- input_grad: float32 [4096, 768], P(('rep', 'shard'))
- grad_ln1_gain: float32 [1, 768], P(None, 'shard')
- grad_ln1_bias: float32 [1, 768], P(None, 'shard')
- grad_qkv_weight: float32 [1, 768, 2304], P(None, 'shard')
- grad_qv_bias: float32 [1, 1536], P(None, 'shard')
- grad_out_weight: float32 [1, 768, 768], P(None, 'shard')
- grad_out_bias: float32 [1, 768], P(None, 'shard')
- grad_ln2_gain: float32 [1, 768], P(None, 'shard')
- grad_ln2_bias: float32 [1, 768], P(None, 'shard')
- grad_fc_weight: float32 [1, 768, 3072], P(None, 'shard')
- grad_fc_bias: float32 [1, 3072], P(None, 'shard')
- grad_proj_weight: float32 [1, 3072, 768], P(None, 'shard')
- grad_proj_bias: float32 [1, 768], P(None, 'shard')
Inputs may be any that keep to these rules, and one draw needn't show every extreme that they name: `segment_ids`: each aligned block of 128 rows (one device's rows) holds three documents with ids 0, 1, 2 in this order, each of one row or more, followed by padding rows of id 3, which attend among themselves; the first block has no padding and the last block is half padding.
All inputs are finite; a program needn't handle non-finite values.
Results may differ from a plain program's by a relative error of at most 0.0098.
Values may be sent and summed in bfloat16 or wider, within the bound.
A program may use at most 128 MiB of HBM per device.

v0:
```python
import jax
import jax.numpy as jnp
from jax import lax
from jax.sharding import PartitionSpec as P

HEADS = 12
HEAD = 64
LAYERS = 1
epsilon = 1e-05


def to_float(value):
    return value.astype(jnp.float32)


def layer_norm(inputs, norm_gain, norm_shift):
    center = inputs - jnp.mean(inputs, axis=-1, keepdims=True)
    inverse_std = lax.rsqrt(jnp.mean(center * center, axis=-1, keepdims=True) + epsilon)
    normed = center * inverse_std
    return (normed * norm_gain + norm_shift, normed, inverse_std)


def norm_back(upstream, normed, inverse_std, norm_gain):
    scaled = upstream * norm_gain
    inner_term = scaled - jnp.mean(scaled, axis=-1, keepdims=True)
    inner_term = inner_term - normed * jnp.mean(scaled * normed, axis=-1, keepdims=True)
    return (inverse_std * inner_term, jnp.sum(upstream * normed, axis=0), jnp.sum(upstream, axis=0))


def layer_forward(inputs, allowed, weights, kept_lse):
    (
        ln1_gain,
        ln1_bias,
        qkv_weight,
        qv_bias,
        out_weight,
        out_bias,
        ln2_gain,
        ln2_bias,
        fc_weight,
        fc_bias,
        proj_weight,
        proj_bias,
    ) = weights
    row_count = inputs.shape[0]
    width_all = inputs.shape[1]
    first_norm, normed_one, inverse_one = layer_norm(inputs, to_float(ln1_gain), to_float(ln1_bias))
    first_low = first_norm.astype(jnp.bfloat16)
    offset = jnp.concatenate(
        [
            to_float(qv_bias[:width_all]),
            jnp.zeros((width_all,), jnp.float32),
            to_float(qv_bias[width_all:]),
        ]
    )
    projected = (
        jnp.dot(first_low, qkv_weight, preferred_element_type=jnp.float32) + offset
    ).astype(jnp.bfloat16)
    queries = projected[:, :width_all].reshape(row_count, HEADS, HEAD)
    keys_all = projected[:, width_all : 2 * width_all].reshape(row_count, HEADS, HEAD)
    values_all = projected[:, 2 * width_all :].reshape(row_count, HEADS, HEAD)
    scores = jnp.einsum(
        "qhd,khd->hqk", queries, keys_all, preferred_element_type=jnp.float32
    ) * HEAD ** (-0.5)
    scores = jnp.where(allowed[None], scores, -1e30)
    if kept_lse is None:
        row_max = jnp.max(scores, axis=-1, keepdims=True)
        log_total = row_max + jnp.log(jnp.sum(jnp.exp(scores - row_max), axis=-1, keepdims=True))
    else:
        log_total = kept_lse
    attn_probs = jnp.exp(scores - log_total)
    probs_low = attn_probs.astype(jnp.bfloat16)
    attn_mixed = jnp.einsum(
        "hqk,khd->qhd", probs_low, values_all, preferred_element_type=jnp.float32
    )
    attn_mixed = attn_mixed.reshape(row_count, width_all).astype(jnp.bfloat16)
    after_attn = (
        inputs
        + jnp.dot(attn_mixed, out_weight, preferred_element_type=jnp.float32)
        + to_float(out_bias)
    )
    second_norm, normed_two, inverse_two = layer_norm(
        after_attn, to_float(ln2_gain), to_float(ln2_bias)
    )
    second_low = second_norm.astype(jnp.bfloat16)
    hidden_pre = jnp.dot(second_low, fc_weight, preferred_element_type=jnp.float32) + to_float(
        fc_bias
    )
    hidden_low = jax.nn.gelu(hidden_pre, approximate=True).astype(jnp.bfloat16)
    result = (
        after_attn
        + jnp.dot(hidden_low, proj_weight, preferred_element_type=jnp.float32)
        + to_float(proj_bias)
    )
    return dict(
        normed_one=normed_one,
        inverse_one=inverse_one,
        first_low=first_low,
        queries=queries,
        keys_all=keys_all,
        values_all=values_all,
        attn_probs=attn_probs,
        probs_low=probs_low,
        attn_mixed=attn_mixed,
        normed_two=normed_two,
        inverse_two=inverse_two,
        second_low=second_low,
        hidden_pre=hidden_pre,
        hidden_low=hidden_low,
        result=result,
        log_total=log_total,
    )


def layer_backward(upstream, saved, weights):
    (
        ln1_gain,
        ln1_bias,
        qkv_weight,
        qv_bias,
        out_weight,
        out_bias,
        ln2_gain,
        ln2_bias,
        fc_weight,
        fc_bias,
        proj_weight,
        proj_bias,
    ) = weights
    row_count = upstream.shape[0]
    width_all = upstream.shape[1]
    proj_in = upstream.astype(jnp.bfloat16)
    grad_proj = jnp.einsum(
        "tf,td->fd", saved["hidden_low"], proj_in, preferred_element_type=jnp.float32
    )
    grad_proj_b = jnp.sum(to_float(proj_in), axis=0)
    hidden_grad = jnp.einsum("td,fd->tf", proj_in, proj_weight, preferred_element_type=jnp.float32)
    _, gelu_pull = jax.vjp(lambda value: jax.nn.gelu(value, approximate=True), saved["hidden_pre"])
    pre_grad = gelu_pull(hidden_grad)[0].astype(jnp.bfloat16)
    grad_fc = jnp.einsum(
        "td,tf->df", saved["second_low"], pre_grad, preferred_element_type=jnp.float32
    )
    grad_fc_b = jnp.sum(to_float(pre_grad), axis=0)
    second_grad = jnp.einsum("tf,df->td", pre_grad, fc_weight, preferred_element_type=jnp.float32)
    norm_part, grad_ln2_g, grad_ln2_b = norm_back(
        second_grad, saved["normed_two"], saved["inverse_two"], to_float(ln2_gain)
    )
    residual_grad = upstream + norm_part
    branch_in = residual_grad.astype(jnp.bfloat16)
    grad_out = jnp.einsum(
        "tc,td->cd", saved["attn_mixed"], branch_in, preferred_element_type=jnp.float32
    )
    grad_out_b = jnp.sum(to_float(branch_in), axis=0)
    mixed_grad = jnp.einsum("td,cd->tc", branch_in, out_weight, preferred_element_type=jnp.float32)
    mixed_grad = mixed_grad.astype(jnp.bfloat16).reshape(row_count, HEADS, HEAD)
    prob_grad = jnp.einsum(
        "qhd,khd->hqk", mixed_grad, saved["values_all"], preferred_element_type=jnp.float32
    )
    value_grad = jnp.einsum(
        "hqk,qhd->khd", saved["probs_low"], mixed_grad, preferred_element_type=jnp.float32
    )
    attn_probs = saved["attn_probs"]
    row_delta = jnp.sum(attn_probs * prob_grad, axis=-1, keepdims=True)
    score_grad = (attn_probs * (prob_grad - row_delta)).astype(jnp.bfloat16)
    query_grad = jnp.einsum(
        "hqk,khd->qhd", score_grad, saved["keys_all"], preferred_element_type=jnp.float32
    ) * HEAD ** (-0.5)
    key_grad = jnp.einsum(
        "hqk,qhd->khd", score_grad, saved["queries"], preferred_element_type=jnp.float32
    ) * HEAD ** (-0.5)
    joined_grad = jnp.concatenate(
        [
            query_grad.reshape(row_count, width_all),
            key_grad.reshape(row_count, width_all),
            value_grad.reshape(row_count, width_all),
        ],
        axis=1,
    ).astype(jnp.bfloat16)
    grad_qkv = jnp.einsum(
        "tc,te->ce", saved["first_low"], joined_grad, preferred_element_type=jnp.float32
    )
    column_sums = jnp.sum(to_float(joined_grad), axis=0)
    grad_qv_b = jnp.concatenate([column_sums[:width_all], column_sums[2 * width_all :]])
    first_grad = jnp.einsum(
        "te,ce->tc", joined_grad, qkv_weight, preferred_element_type=jnp.float32
    )
    norm_first, grad_ln1_g, grad_ln1_b = norm_back(
        first_grad, saved["normed_one"], saved["inverse_one"], to_float(ln1_gain)
    )
    gradients = (
        grad_ln1_g,
        grad_ln1_b,
        grad_qkv,
        grad_qv_b,
        grad_out,
        grad_out_b,
        grad_ln2_g,
        grad_ln2_b,
        grad_fc,
        grad_fc_b,
        grad_proj,
        grad_proj_b,
    )
    return (residual_grad + norm_first, gradients)


def own_grads(gradients):
    shares = (
        lax.psum_scatter(gradients[0], "shard", scatter_dimension=0, tiled=True),
        lax.psum_scatter(gradients[1], "shard", scatter_dimension=0, tiled=True),
        lax.psum_scatter(gradients[2], "shard", scatter_dimension=0, tiled=True),
        lax.psum_scatter(gradients[3], "shard", scatter_dimension=0, tiled=True),
        lax.psum_scatter(gradients[4], "shard", scatter_dimension=0, tiled=True),
        lax.psum_scatter(gradients[5], "shard", scatter_dimension=0, tiled=True),
        lax.psum_scatter(gradients[6], "shard", scatter_dimension=0, tiled=True),
        lax.psum_scatter(gradients[7], "shard", scatter_dimension=0, tiled=True),
        lax.psum_scatter(gradients[8], "shard", scatter_dimension=0, tiled=True),
        lax.psum_scatter(gradients[9], "shard", scatter_dimension=0, tiled=True),
        lax.psum_scatter(gradients[10], "shard", scatter_dimension=0, tiled=True),
        lax.psum_scatter(gradients[11], "shard", scatter_dimension=0, tiled=True),
    )
    owned = lax.psum(
        (
            shares[0],
            shares[1],
            shares[2],
            shares[3],
            shares[4],
            shares[5],
            shares[6],
            shares[7],
            shares[8],
            shares[9],
            shares[10],
            shares[11],
        ),
        "rep",
    )
    return owned


def per_device(
    tokens,
    segment_ids,
    cotangent,
    ln1_gain,
    ln1_bias,
    qkv_weight,
    qv_bias,
    out_weight,
    out_bias,
    ln2_gain,
    ln2_bias,
    fc_weight,
    fc_bias,
    proj_weight,
    proj_bias,
):
    row_count = tokens.shape[0]
    positions = jnp.arange(row_count)
    allowed = (segment_ids[:, None] == segment_ids[None, :]) & (
        positions[None, :] <= positions[:, None]
    )
    residual = to_float(tokens)
    layer_index = 0
    gathered = (
        lax.all_gather(ln1_gain[layer_index], "shard", axis=0, tiled=True),
        lax.all_gather(ln1_bias[layer_index], "shard", axis=0, tiled=True),
        lax.all_gather(qkv_weight[layer_index], "shard", axis=0, tiled=True),
        lax.all_gather(qv_bias[layer_index], "shard", axis=0, tiled=True),
        lax.all_gather(out_weight[layer_index], "shard", axis=0, tiled=True),
        lax.all_gather(out_bias[layer_index], "shard", axis=0, tiled=True),
        lax.all_gather(ln2_gain[layer_index], "shard", axis=0, tiled=True),
        lax.all_gather(ln2_bias[layer_index], "shard", axis=0, tiled=True),
        lax.all_gather(fc_weight[layer_index], "shard", axis=0, tiled=True),
        lax.all_gather(fc_bias[layer_index], "shard", axis=0, tiled=True),
        lax.all_gather(proj_weight[layer_index], "shard", axis=0, tiled=True),
        lax.all_gather(proj_bias[layer_index], "shard", axis=0, tiled=True),
    )
    saved = layer_forward(residual, allowed, gathered, None)
    kept_inputs = [residual]
    kept_lse = [saved["log_total"]]
    residual = saved["result"]
    out_tokens = residual.astype(jnp.bfloat16)
    upstream = to_float(cotangent)
    owned_grads = [None] * LAYERS
    for layer_index in reversed(range(LAYERS)):
        gathered = (
            lax.all_gather(ln1_gain[layer_index], "shard", axis=0, tiled=True),
            lax.all_gather(ln1_bias[layer_index], "shard", axis=0, tiled=True),
            lax.all_gather(qkv_weight[layer_index], "shard", axis=0, tiled=True),
            lax.all_gather(qv_bias[layer_index], "shard", axis=0, tiled=True),
            lax.all_gather(out_weight[layer_index], "shard", axis=0, tiled=True),
            lax.all_gather(out_bias[layer_index], "shard", axis=0, tiled=True),
            lax.all_gather(ln2_gain[layer_index], "shard", axis=0, tiled=True),
            lax.all_gather(ln2_bias[layer_index], "shard", axis=0, tiled=True),
            lax.all_gather(fc_weight[layer_index], "shard", axis=0, tiled=True),
            lax.all_gather(fc_bias[layer_index], "shard", axis=0, tiled=True),
            lax.all_gather(proj_weight[layer_index], "shard", axis=0, tiled=True),
            lax.all_gather(proj_bias[layer_index], "shard", axis=0, tiled=True),
        )
        saved = layer_forward(kept_inputs[layer_index], allowed, gathered, kept_lse[layer_index])
        upstream, gradients = layer_backward(upstream, saved, gathered)
        owned_grads[layer_index] = own_grads(gradients)
    stacked = tuple((jnp.stack([owned_grads[0][member]]) for member in range(12)))
    return (out_tokens, upstream) + stacked


def solution(mesh):
    placed = (
        P(("rep", "shard"), None),
        P(("rep", "shard")),
        P(("rep", "shard"), None),
        P(None, "shard"),
        P(None, "shard"),
        P(None, "shard", None),
        P(None, "shard"),
        P(None, "shard", None),
        P(None, "shard"),
        P(None, "shard"),
        P(None, "shard"),
        P(None, "shard", None),
        P(None, "shard"),
        P(None, "shard", None),
        P(None, "shard"),
    )
    return jax.shard_map(
        per_device,
        mesh=mesh,
        in_specs=placed,
        out_specs=(
            P(("rep", "shard"), None),
            P(("rep", "shard"), None),
            P(None, "shard"),
            P(None, "shard"),
            P(None, "shard", None),
            P(None, "shard"),
            P(None, "shard", None),
            P(None, "shard"),
            P(None, "shard"),
            P(None, "shard"),
            P(None, "shard", None),
            P(None, "shard"),
            P(None, "shard", None),
            P(None, "shard"),
        ),
        check_vma=False,
    )
```

profile of v0, /device:TPU:0, one launch (start us, length us, event | category | flops | bytes accessed | tf_op | source)
XLA Modules:
  0.0 913.5 jit_solution(14599363228877090021)
XLA Ops:
  13.7 39.5 %all-reduce.18 = (bf16[1536]{0:T(1024)(128)(2,1)S(1)}, bf16[768]{0:T(1024)(128)(2,1)S(1)}, bf16[768]{0:T(1024)(128)(2,1)S(1)}, bf16[768]{0:T(1024)(128)(2,1)S(1)...) all-reduce(bf16[1536]{0:T(1024)(128)(2,1)S(1)} %dynamic-update-slic, ...), channel_id=5, replica_groups=mesh['rep'=4,'shard'=8] {'shard'}, use_global_device_ids=true, to_apply=%add.2 | all-reduce | flops 6144 | bytes 24576
  53.3 26.1 %all-gather.9 = bf16[1,3072]{1,0:T(2,128)(2,1)S(1)} all-gather(bf16[1,384]{1,0:T(2,128)(2,1)S(1)} %copy-done.39), channel_id=11, replica_groups=mesh['rep'=4,'shard'=8] {'shard'}, dimensions={1}, use_global_device_ids=true | all-gather | bytes 6912 | tf_op jit(solution)/shard_map/all_gather | solution.py:276
  80.0 2.7 fusion.11
  84.0 36.8 %all-gather.19.cloned.1.call-done = bf16[1,768,768]{2,1,0:T(8,128)(2,1)} async-done(((bf16[1,96,768]{2,1,0:T(8,128)(2,1)}), bf16[1,768,768]{2,1,0:T(8,128)(2,1)}) %all-gather.19.cloned.1.call-update) | async-done | bytes 1179664 | tf_op jit(solution)/shard_map/all_gather | solution.py:271
  120.8 1.7 fusion.75
  122.8 78.9 %all-gather.21.cloned.1.call-done = bf16[1,768,3072]{2,1,0:T(8,128)(2,1)} async-done(((bf16[1,96,3072]{2,1,0:T(8,128)(2,1)}), bf16[1,768,3072]{2,1,0:T(8,128)(2,1)}) %all-gather.21.cloned.1.call-update) | async-done | bytes 4718608 | tf_op jit(solution)/shard_map/all_gather | solution.py:275
  201.7 3.2 fusion.8
  204.9 76.8 %all-gather.23.cloned.1.call-done = bf16[1,3072,768]{2,1,0:T(8,128)(2,1)} async-done(((bf16[1,384,768]{2,1,0:T(8,128)(2,1)}), bf16[1,3072,768]{2,1,0:T(8,128)(2,1)}) %all-gather.23.cloned.1.call-update) | async-done | bytes 4718608 | tf_op jit(solution)/shard_map/all_gather | solution.py:277
  281.8 5.0 convert_reduce_fusion
  286.9 2.3 multiply_reduce_fusion.1
  289.2 1.5 convert_reduce_fusion.4
  290.7 1.8 fusion.63
  292.8 2.5 fusion.35
  295.3 1.7 copy.53
  297.0 1.3 multiply_reduce_fusion
  300.2 4.1 fusion.66
  304.4 1.1 copy-done.3
  305.5 5.8 fusion.69
  311.4 0.9 copy-done.19
  312.2 5.2 fusion.70
  320.9 4.1 fusion.56
  324.9 35.8 %all-reduce.15 = (f32[768]{0:T(1024)S(1)}, f32[768]{0:T(1024)S(1)}, f32[1536]{0:T(1024)S(1)}, f32[768]{0:T(1024)S(1)}, f32[768]{0:T(1024)S(1)}, /*index=5*/f32[7...) all-reduce(f32[768]{0:T(1024)} %get-tuple-element.16, ...), channel_id=14, replica_groups=mesh['rep'=4,'shard'=8] {'shard'}, use_global_device_ids=true, to_apply=%region_12.13.clone | all-reduce | flops 9216 | bytes 73728
  360.8 130.8 %reduce-scatter.5.cloned.1.call-done = f32[96,2304]{1,0:T(8,128)} async-done(((f32[768,2304]{1,0:T(8,128)}), f32[96,2304]{1,0:T(8,128)}) %reduce-scatter.5.cloned.1.call-update) | async-done | bytes 884752 | tf_op jit(solution)/shard_map/reduce_scatter | solution.py:211
  491.5 166.6 %reduce-scatter.9.cloned.1.call-done = f32[96,3072]{1,0:T(8,128)} async-done(((f32[768,3072]{1,0:T(8,128)}), f32[96,3072]{1,0:T(8,128)}) %reduce-scatter.9.cloned.1.call-update) | async-done | bytes 1179664 | tf_op jit(solution)/shard_map/reduce_scatter | solution.py:217
  658.1 166.6 %reduce-scatter.11.cloned.1.call-done = f32[384,768]{1,0:T(8,128)} async-done(((f32[3072,768]{1,0:T(8,128)}), f32[384,768]{1,0:T(8,128)}) %reduce-scatter.11.cloned.1.call-update) | async-done | bytes 1179664 | tf_op jit(solution)/shard_map/reduce_scatter | solution.py:219
  825.3 7.5 all-reduce.16
  832.9 0.9 fusion.55
  833.8 4.1 fusion.38
  837.9 64.1 %all-reduce.21.cloned.1.call-done = (f32[1,96,2304]{2,1,0:T(8,128)}, f32[1,96,768]{2,1,0:T(8,128)}, f32[1,96,3072]{2,1,0:T(8,128)}, f32[1,384,768]{2,1,0:T(8,128)}) async-done(((f32[1,96,2304]{2,1,0:T(8,128)}, f32[1,96,768]{2,1,0:T(8,128)}, f32[1,96,3072]{2,1,0:T(8,128)}, f32[1,384,768]{2,1,0:T(8,128)}), (f32[1,96,2304]{2,1,0:T(8,128)}, f32[1,96,768]{2,1,0:T(8,128)}, f32[1,96,3072]{2,1,0:T(8,128)}, ...) | async-done | bytes 3538960 | tf_op jit(solution)/shard_map/psum | solution.py:222
  902.0 2.2 copy.72
  905.0 1.0 copy.74
  906.0 1.0 copy.75
  (179 shorter events, 12.1 us)
Async XLA Ops:
  7.2 4.8 copy-start.40
  7.2 4.9 copy-start.41
  7.2 5.1 copy-start.42
  7.2 5.3 copy-start.43
  7.2 5.6 copy-start.44
  7.2 5.8 copy-start.45
  7.3 6.0 copy-start.46
  7.3 46.0 %copy-start.39 = (bf16[1,384]{1,0:T(2,128)(2,1)S(1)}, bf16[1,384]{1,0:T(2,128)(2,1)}, u32[]{:S(2)}) copy-start(bf16[1,384]{1,0:T(2,128)(2,1)} %param.27) | copy-start | bytes 2308
  7.3 72.2 %copy-start.1 = (bf16[128,768]{1,0:T(8,128)(2,1)S(1)}, bf16[128,768]{1,0:T(8,128)(2,1)}, u32[]{:S(2)}) copy-start(bf16[128,768]{1,0:T(8,128)(2,1)} %param.15) | copy-start | bytes 589828
  7.3 72.5 %copy-start.37 = (s32[128]{0:T(128)S(1)}, s32[128]{0:T(128)}, u32[]{:S(2)}) copy-start(s32[128]{0:T(128)} %param.16) | copy-start | bytes 1540
  7.3 72.7 %all-gather.17.cloned.1.call-start = ((), (), s32[]{:S(2)}) async-start(), calls=%async_computation.8 | async-start | bytes 3981312 | tf_op jit(solution)/shard_map/all_gather | solution.py:269
  8.0 112.8 %all-gather.19.cloned.1.call-start = ((), (), s32[]{:S(2)}) async-start(), calls=%async_computation.9 | async-start | bytes 1327104 | tf_op jit(solution)/shard_map/all_gather | solution.py:271
  8.8 192.9 %all-gather.21.cloned.1.call-start = ((), (), s32[]{:S(2)}) async-start(), calls=%async_computation.10 | async-start | bytes 5308416 | tf_op jit(solution)/shard_map/all_gather | solution.py:275
  9.5 272.3 %all-gather.23.cloned.1.call-start = ((), (), s32[]{:S(2)}) async-start(), calls=%async_computation.11 | async-start | bytes 5308416 | tf_op jit(solution)/shard_map/all_gather | solution.py:277
  10.1 350.7 %reduce-scatter.7.cloned.1.call-start = ((), (), s32[]{:S(2)}) async-start(), calls=%async_computation.5 | async-start | bytes 2654208 | tf_op jit(solution)/shard_map/reduce_scatter | solution.py:213
  53.3 29.4 %copy-start.23 = (f32[768]{0:T(1024)}, f32[768]{0:T(1024)S(1)}, u32[]{:S(2)}) copy-start(f32[768]{0:T(1024)S(1)} %convert_element_type.137) | copy-start | bytes 9220
  79.4 122.3 %copy-start.21 = (f32[768]{0:T(1024)}, f32[768]{0:T(1024)S(1)}, u32[]{:S(2)}) copy-start(f32[768]{0:T(1024)S(1)} %convert_element_type.140) | copy-start | bytes 9220
  122.6 164.3 %copy-start.25 = (f32[128]{0:T(128)}, f32[128]{0:T(128)S(1)}, u32[]{:S(2)}) copy-start(f32[128]{0:T(128)S(1)} %broadcast_multiply_fusion.4) | copy-start | bytes 1540
  122.8 164.1 %copy-start.31 = (f32[128]{0:T(128)}, f32[128]{0:T(128)S(1)}, u32[]{:S(2)}) copy-start(f32[128]{0:T(128)S(1)} %add_rsqrt_fusion) | copy-start | bytes 1540
  201.7 80.1 %copy-start.17 = (bf16[128,768]{1,0:T(8,128)(2,1)S(1)}, bf16[128,768]{1,0:T(8,128)(2,1)}, u32[]{:S(2)}) copy-start(bf16[128,768]{1,0:T(8,128)(2,1)} %param.17) | copy-start | bytes 589828
  281.8 5.0 copy-start
  292.5 4.5 copy-start.9
  292.5 199.0 %reduce-scatter.5.cloned.1.call-start = ((), (), s32[]{:S(2)}) async-start(), calls=%async_computation.4 | async-start | bytes 7962624 | tf_op jit(solution)/shard_map/reduce_scatter | solution.py:211
  304.4 353.7 %reduce-scatter.9.cloned.1.call-start = ((), (), s32[]{:S(2)}) async-start(), calls=%async_computation.6 | async-start | bytes 10616832 | tf_op jit(solution)/shard_map/reduce_scatter | solution.py:217
  311.3 513.4 %reduce-scatter.11.cloned.1.call-start = ((), (), s32[]{:S(2)}) async-start(), calls=%async_computation.7 | async-start | bytes 10616832 | tf_op jit(solution)/shard_map/reduce_scatter | solution.py:219
  317.4 584.5 %all-reduce.21.cloned.1.call-start = ((), (), s32[]{:S(2)}) async-start(), calls=%async_computation.12 | async-start | bytes 7077888 | tf_op jit(solution)/shard_map/psum | solution.py:222
  320.9 4.1 copy-start.27
  824.7 8.2 copy-start.48
  824.7 8.2 copy-start.47
  824.7 8.2 copy-start.30
  824.7 8.2 copy-start.34
  824.7 9.1 copy-start.35
  (26 other events, 44.6 us)
Sparse Core Ops, SparseCore 0:
  10.3 68.5 all-gather.16
  81.1 39.6 all-gather.18
  123.0 78.6 all-gather.20
  203.7 78.0 all-gather.22
  292.6 67.2 reduce-scatter.6
  363.5 128.0 reduce-scatter.4
  495.5 162.4 reduce-scatter.8
  662.1 162.5 reduce-scatter.10
  827.4 74.4 all-reduce.20
where the time goes:
time: 914 us
  waiting for transfers between devices  723 us (79%)
  blocking collectives  109 us (12%)
  matrix products  45.5 us (5%)
  between operations  17.8 us (2%)
  local copies, waits for them, and re-layouts  13.4 us (1%)
    reduce_scatter x1, waiting for transfers between devices, own_grads(): lax.psum_scatter(gradients[10], 'shard', scatter_dimension=0, tiled=True)  167 us
    reduce_scatter x1, waiting for transfers between devices, own_grads(): lax.psum_scatter(gradients[8], 'shard', scatter_dimension=0, tiled=True)  167 us
    reduce_scatter x1, waiting for transfers between devices, own_grads(): lax.psum_scatter(gradients[2], 'shard', scatter_dimension=0, tiled=True)  131 us
    all_gather x1, waiting for transfers between devices, per_device(): lax.all_gather(fc_weight[layer_index], 'shard', axis=0, tiled=True)  78.9 us
    all_gather x1, waiting for transfers between devices, per_device(): lax.all_gather(proj_weight[layer_index], 'shard', axis=0, tiled=True)  76.8 us
    unnamed x2, blocking collectives  75.3 us
    psum x1, waiting for transfers between devices, own_grads(): lax.psum((shares[0], shares[1], shares[2], shares[3], shares[4], shares[5...  64.1 us
    all_gather x1, waiting for transfers between devices, per_device(): lax.all_gather(out_weight[layer_index], 'shard', axis=0, tiled=True)  36.8 us
  transfers between devices with their start and end apart: 9, of which 7 were waited for; matrix products, arithmetic and copies ran while one was open for 5% of the time, Pallas kernels for 0%

commit v1 on v0

--- a/solution.py
+++ b/solution.py
@@ -7,6 +7,27 @@
 HEAD = 64
 LAYERS = 1
 epsilon = 1e-05
+
+
+def collect(array, axis, dim):
+    peers, index, extent = (lax.axis_size(axis), lax.axis_index(axis), array.shape[dim])
+    right = [(i, (i + 1) % peers) for i in range(peers)]
+    left = [(i, (i - 1) % peers) for i in range(peers)]
+    filled = jnp.zeros((*array.shape[:dim], peers * extent, *array.shape[dim + 1 :]), array.dtype)
+    filled = lax.dynamic_update_slice_in_dim(filled, array, index * extent, axis=dim)
+    from_left = from_right = array
+    middle = peers // 2
+    for step in range(1, middle + 1):
+        from_left = lax.ppermute(from_left, axis, right)
+        filled = lax.dynamic_update_slice_in_dim(
+            filled, from_left, (index - step) % peers * extent, axis=dim
+        )
+        if step < peers - middle:
+            from_right = lax.ppermute(from_right, axis, left)
+            filled = lax.dynamic_update_slice_in_dim(
+                filled, from_right, (index + step) % peers * extent, axis=dim
+            )
+    return filled
 
 
 def to_float(value):
@@ -274,7 +295,7 @@
         lax.all_gather(ln2_bias[layer_index], "shard", axis=0, tiled=True),
         lax.all_gather(fc_weight[layer_index], "shard", axis=0, tiled=True),
         lax.all_gather(fc_bias[layer_index], "shard", axis=0, tiled=True),
-        lax.all_gather(proj_weight[layer_index], "shard", axis=0, tiled=True),
+        collect(proj_weight[layer_index], "shard", 0),
         lax.all_gather(proj_bias[layer_index], "shard", axis=0, tiled=True),
     )
     saved = layer_forward(residual, allowed, gathered, None)

time: 914 us -> 962 us (1.053)
  waiting for transfers between devices: 723 us -> 750 us
  starting transfers between devices: 0.54 us -> 16.7 us
    ppermute x0 -> x7, waiting for transfers between devices: none -> 86.8 us  [the longest x4 56.6 us: collect(): from_left = lax.ppermute(from_left, axis, right)]
    reduce_scatter x1, waiting for transfers between devices: 131 us -> 70.4 us  [own_grads(): lax.psum_scatter(gradients[2], 'shard', scatter_dimension=0, tiled=True)]
    ppermute x0 -> x7, starting transfers between devices: none -> 16.2 us  [the longest x3 13.1 us: collect(): from_right = lax.ppermute(from_right, axis, left)]
  transfers between devices with their start and end apart: 9 -> 16, of which waited for: 7 -> 13; matrix products, arithmetic and copies ran while one was open for 5% -> 5% of each run, Pallas kernels for 0% -> 0%
where the time goes in v1:
time: 962 us; the launch traced here: 961 us
  waiting for transfers between devices  750 us (78%)
  blocking collectives  111 us (12%)
  matrix products  42.9 us (4%)
  local copies, waits for them, and re-layouts  19.4 us (2%)
  between operations  17.9 us (2%)
  starting transfers between devices  16.7 us (2%)
    reduce_scatter x1, waiting for transfers between devices, own_grads(): lax.psum_scatter(gradients[10], 'shard', scatter_dimension=0, tiled=True)  166 us
    reduce_scatter x1, waiting for transfers between devices, own_grads(): lax.psum_scatter(gradients[8], 'shard', scatter_dimension=0, tiled=True)  166 us
    all_gather x1, waiting for transfers between devices, per_device(): lax.all_gather(fc_weight[layer_index], 'shard', axis=0, tiled=True)  78.9 us
    unnamed x2, blocking collectives  77.8 us
    all_gather x1, waiting for transfers between devices, per_device(): lax.all_gather(proj_weight[layer_index], 'shard', axis=0, tiled=True)  76.8 us
    reduce_scatter x1, waiting for transfers between devices, own_grads(): lax.psum_scatter(gradients[2], 'shard', scatter_dimension=0, tiled=True)  70.4 us
    psum x1, waiting for transfers between devices, own_grads(): lax.psum((shares[0], shares[1], shares[2], shares[3], shares[4], shares[5...  64.2 us
    ppermute x4, waiting for transfers between devices, collect(): from_left = lax.ppermute(from_left, axis, right)  56.6 us
  transfers between devices with their start and end apart: 16, of which 13 were waited for; matrix products, arithmetic and copies ran while one was open for 5% of the time, Pallas kernels for 0%

profile of v1, /device:TPU:0, one launch (start us, length us, event | category | flops | bytes accessed | tf_op | source)
XLA Modules:
  0.0 961.4 jit_solution(3826830733126293712)
XLA Ops:
  13.7 39.5 %all-reduce.18 = (bf16[1536]{0:T(1024)(128)(2,1)S(1)}, bf16[768]{0:T(1024)(128)(2,1)S(1)}, bf16[768]{0:T(1024)(128)(2,1)S(1)}, bf16[768]{0:T(1024)(128)(2,1)S(1)...) all-reduce(bf16[1536]{0:T(1024)(128)(2,1)S(1)} %dynamic-update-slic, ...), channel_id=5, replica_groups=mesh['rep'=4,'shard'=8] {'shard'}, use_global_device_ids=true, to_apply=%add.2 | all-reduce | flops 6144 | bytes 24576
  53.3 26.1 %all-gather.9 = bf16[1,3072]{1,0:T(2,128)(2,1)S(1)} all-gather(bf16[1,384]{1,0:T(2,128)(2,1)S(1)} %copy-done.47), channel_id=11, replica_groups=mesh['rep'=4,'shard'=8] {'shard'}, dimensions={1}, use_global_device_ids=true | all-gather | bytes 6912 | tf_op jit(solution)/shard_map/all_gather | solution.py:297
  80.0 2.7 fusion.9
  84.0 36.7 %all-gather.19.cloned.1.call-done = bf16[1,768,768]{2,1,0:T(8,128)(2,1)} async-done(((bf16[1,96,768]{2,1,0:T(8,128)(2,1)}), bf16[1,768,768]{2,1,0:T(8,128)(2,1)}) %all-gather.19.cloned.1.call-update) | async-done | bytes 1179664 | tf_op jit(solution)/shard_map/all_gather | solution.py:292
  122.7 78.9 %all-gather.21.cloned.1.call-done = bf16[1,768,3072]{2,1,0:T(8,128)(2,1)} async-done(((bf16[1,96,3072]{2,1,0:T(8,128)(2,1)}), bf16[1,768,3072]{2,1,0:T(8,128)(2,1)}) %all-gather.21.cloned.1.call-update) | async-done | bytes 4718608 | tf_op jit(solution)/shard_map/all_gather | solution.py:296
  201.7 3.2 fusion.6
  204.9 76.8 %all-gather.23.cloned.1.call-done = bf16[1,3072,768]{2,1,0:T(8,128)(2,1)} async-done(((bf16[1,384,768]{2,1,0:T(8,128)(2,1)}), bf16[1,3072,768]{2,1,0:T(8,128)(2,1)}) %all-gather.23.cloned.1.call-update) | async-done | bytes 4718608 | tf_op jit(solution)/shard_map/all_gather | solution.py:320
  281.8 5.0 convert_reduce_fusion
  286.8 2.3 multiply_reduce_fusion.1
  290.6 1.9 fusion.54
  292.8 2.5 fusion.29
  300.2 4.1 fusion.57
  305.5 5.8 fusion.60
  312.2 5.2 fusion.61
  319.0 4.2 collective-permute-start.1
  323.2 26.4 %collective-permute-done = bf16[384,768]{1,0:T(8,128)(2,1)S(1)} collective-permute-done((bf16[384,768]{1,0:T(8,128)(2,1)S(1)}, bf16[384,768]{1,0:T(8,128)(2,1)S(1)}, u32[]{:S(2)}, u32[]{:S(2)}) %collective-permute-start) | collective-permute-done | bytes 589856 | tf_op jit(solution)/shard_map/ppermute | solution.py:21
  349.6 2.5 collective-permute-start.2
  352.1 2.8 collective-permute-start.3
  354.9 12.2 %collective-permute-done.2 = bf16[384,768]{1,0:T(8,128)(2,1)} collective-permute-done((bf16[384,768]{1,0:T(8,128)(2,1)S(1)}, bf16[384,768]{1,0:T(8,128)(2,1)}, u32[]{:S(2)}, u32[]{:S(2)}) %collective-permute-start.2) | collective-permute-done | bytes 589856 | tf_op jit(solution)/shard_map/ppermute | solution.py:21
  369.5 11.4 %collective-permute-done.3 = bf16[384,768]{1,0:T(8,128)(2,1)} collective-permute-done((bf16[384,768]{1,0:T(8,128)(2,1)}, bf16[384,768]{1,0:T(8,128)(2,1)}, u32[]{:S(2)}, u32[]{:S(2)}) %collective-permute-start.3) | collective-permute-done | bytes 589856 | tf_op jit(solution)/shard_map/ppermute | solution.py:26
  380.9 6.1 collective-permute-start.5
  387.1 13.6 %collective-permute-done.4 = bf16[384,768]{1,0:T(8,128)(2,1)} collective-permute-done((bf16[384,768]{1,0:T(8,128)(2,1)}, bf16[384,768]{1,0:T(8,128)(2,1)}, u32[]{:S(2)}, u32[]{:S(2)}) %collective-permute-start.4) | collective-permute-done | bytes 589856 | tf_op jit(solution)/shard_map/ppermute | solution.py:21
  405.4 18.8 %collective-permute-done.5 = bf16[384,768]{1,0:T(8,128)(2,1)S(1)} collective-permute-done((bf16[384,768]{1,0:T(8,128)(2,1)}, bf16[384,768]{1,0:T(8,128)(2,1)S(1)}, u32[]{:S(2)}, u32[]{:S(2)}) %collective-permute-start.5) | collective-permute-done | bytes 589856 | tf_op jit(solution)/shard_map/ppermute | solution.py:26
  424.2 4.5 collective-permute-done.6
  431.0 38.2 %all-reduce.15 = (f32[768]{0:T(1024)S(1)}, f32[768]{0:T(1024)S(1)}, f32[1536]{0:T(1024)S(1)}, f32[768]{0:T(1024)S(1)}, f32[768]{0:T(1024)S(1)}, /*index=5*/f32[7...) all-reduce(f32[768]{0:T(1024)S(1)} %get-tuple-element.16, ...), channel_id=14, replica_groups=mesh['rep'=4,'shard'=8] {'shard'}, use_global_device_ids=true, to_apply=%region_12.13.clone | all-reduce | flops 9216 | bytes 73728
  469.3 70.4 %reduce-scatter.5.cloned.1.call-done = f32[96,2304]{1,0:T(8,128)} async-done(((f32[768,2304]{1,0:T(8,128)}), f32[96,2304]{1,0:T(8,128)}) %reduce-scatter.5.cloned.1.call-update) | async-done | bytes 884752 | tf_op jit(solution)/shard_map/reduce_scatter | solution.py:232
  539.7 166.4 %reduce-scatter.9.cloned.1.call-done = f32[96,3072]{1,0:T(8,128)} async-done(((f32[768,3072]{1,0:T(8,128)}), f32[96,3072]{1,0:T(8,128)}) %reduce-scatter.9.cloned.1.call-update) | async-done | bytes 1179664 | tf_op jit(solution)/shard_map/reduce_scatter | solution.py:238
  706.1 166.5 %reduce-scatter.11.cloned.1.call-done = f32[384,768]{1,0:T(8,128)} async-done(((f32[3072,768]{1,0:T(8,128)}), f32[384,768]{1,0:T(8,128)}) %reduce-scatter.11.cloned.1.call-update) | async-done | bytes 1179664 | tf_op jit(solution)/shard_map/reduce_scatter | solution.py:240
  873.2 7.5 all-reduce.16
  881.6 4.1 fusion.28
  885.6 64.2 %all-reduce.21.cloned.1.call-done = (f32[1,96,2304]{2,1,0:T(8,128)}, f32[1,96,768]{2,1,0:T(8,128)}, f32[1,96,3072]{2,1,0:T(8,128)}, f32[1,384,768]{2,1,0:T(8,128)}) async-done(((f32[1,96,2304]{2,1,0:T(8,128)}, f32[1,96,768]{2,1,0:T(8,128)}, f32[1,96,3072]{2,1,0:T(8,128)}, f32[1,384,768]{2,1,0:T(8,128)}), (f32[1,96,2304]{2,1,0:T(8,128)}, f32[1,96,768]{2,1,0:T(8,128)}, f32[1,96,3072]{2,1,0:T(8,128)}, ...) | async-done | bytes 3538960 | tf_op jit(solution)/shard_map/psum | solution.py:243
  949.9 2.2 copy.80
  (214 shorter events, 30.6 us)
Async XLA Ops:
  7.3 6.0 copy-start.54
  7.3 46.1 %copy-start.47 = (bf16[1,384]{1,0:T(2,128)(2,1)S(1)}, bf16[1,384]{1,0:T(2,128)(2,1)}, u32[]{:S(2)}) copy-start(bf16[1,384]{1,0:T(2,128)(2,1)} %param.27) | copy-start | bytes 2308
  7.3 72.2 %copy-start.1 = (bf16[128,768]{1,0:T(8,128)(2,1)S(1)}, bf16[128,768]{1,0:T(8,128)(2,1)}, u32[]{:S(2)}) copy-start(bf16[128,768]{1,0:T(8,128)(2,1)} %param.15) | copy-start | bytes 589828
  7.3 72.6 %copy-start.45 = (s32[128]{0:T(128)S(1)}, s32[128]{0:T(128)}, u32[]{:S(2)}) copy-start(s32[128]{0:T(128)} %param.16) | copy-start | bytes 1540
  7.3 72.7 %all-gather.17.cloned.1.call-start = ((), (), s32[]{:S(2)}) async-start(), calls=%async_computation.8 | async-start | bytes 3981312 | tf_op jit(solution)/shard_map/all_gather | solution.py:290
  8.0 112.8 %all-gather.19.cloned.1.call-start = ((), (), s32[]{:S(2)}) async-start(), calls=%async_computation.9 | async-start | bytes 1327104 | tf_op jit(solution)/shard_map/all_gather | solution.py:292
  8.8 192.9 %all-gather.21.cloned.1.call-start = ((), (), s32[]{:S(2)}) async-start(), calls=%async_computation.10 | async-start | bytes 5308416 | tf_op jit(solution)/shard_map/all_gather | solution.py:296
  9.5 272.2 %all-gather.23.cloned.1.call-start = ((), (), s32[]{:S(2)}) async-start(), calls=%async_computation.11 | async-start | bytes 5308416 | tf_op jit(solution)/shard_map/all_gather | solution.py:320
  10.1 459.2 %reduce-scatter.7.cloned.1.call-start = ((), (), s32[]{:S(2)}) async-start(), calls=%async_computation.5 | async-start | bytes 2654208 | tf_op jit(solution)/shard_map/reduce_scatter | solution.py:234
  53.3 29.4 %copy-start.28 = (f32[768]{0:T(1024)}, f32[768]{0:T(1024)S(1)}, u32[]{:S(2)}) copy-start(f32[768]{0:T(1024)S(1)} %convert_element_type.137) | copy-start | bytes 9220
  79.4 122.3 %copy-start.26 = (f32[768]{0:T(1024)}, f32[768]{0:T(1024)S(1)}, u32[]{:S(2)}) copy-start(f32[768]{0:T(1024)S(1)} %convert_element_type.140) | copy-start | bytes 9220
  122.5 164.3 %copy-start.30 = (f32[128]{0:T(128)}, f32[128]{0:T(128)S(1)}, u32[]{:S(2)}) copy-start(f32[128]{0:T(128)S(1)} %broadcast_multiply_fusion.4) | copy-start | bytes 1540
  122.7 164.1 %copy-start.39 = (f32[128]{0:T(128)}, f32[128]{0:T(128)S(1)}, u32[]{:S(2)}) copy-start(f32[128]{0:T(128)S(1)} %add_rsqrt_fusion) | copy-start | bytes 1540
  201.7 80.1 %copy-start.20 = (bf16[128,768]{1,0:T(8,128)(2,1)S(1)}, bf16[128,768]{1,0:T(8,128)(2,1)}, u32[]{:S(2)}) copy-start(bf16[128,768]{1,0:T(8,128)(2,1)} %param.17) | copy-start | bytes 589828
  292.5 247.2 %reduce-scatter.5.cloned.1.call-start = ((), (), s32[]{:S(2)}) async-start(), calls=%async_computation.4 | async-start | bytes 7962624 | tf_op jit(solution)/shard_map/reduce_scatter | solution.py:232
  304.4 401.7 %reduce-scatter.9.cloned.1.call-start = ((), (), s32[]{:S(2)}) async-start(), calls=%async_computation.6 | async-start | bytes 10616832 | tf_op jit(solution)/shard_map/reduce_scatter | solution.py:238
  311.3 561.2 %reduce-scatter.11.cloned.1.call-start = ((), (), s32[]{:S(2)}) async-start(), calls=%async_computation.7 | async-start | bytes 10616832 | tf_op jit(solution)/shard_map/reduce_scatter | solution.py:240
  317.4 49.7 %copy-start.44 = (bf16[768]{0:T(1024)(128)(2,1)S(1)}, bf16[768]{0:T(1024)(128)(2,1)}, u32[]{:S(2)}) copy-start(bf16[768]{0:T(1024)(128)(2,1)} %get-tuple-element.48) | copy-start | bytes 4612
  317.5 632.4 %all-reduce.21.cloned.1.call-start = ((), (), s32[]{:S(2)}) async-start(), calls=%async_computation.12 | async-start | bytes 7077888 | tf_op jit(solution)/shard_map/psum | solution.py:243
  318.5 31.1 %collective-permute-start = (bf16[384,768]{1,0:T(8,128)(2,1)S(1)}, bf16[384,768]{1,0:T(8,128)(2,1)S(1)}, u32[]{:S(2)}, u32[]{:S(2)}) collective-permute-start(bf16[384,768]{1,0:T(8,128)(2,1)S(1)} %bitcast.94), channel_id=1, source_target_pairs={{0,1},{1,2},{2,3},{3,4},{4,5},{5,6},{6,7},{7,0},{8,9},{9,10},{10,1... | collective-permute-start | bytes 1769480 | tf_op jit(solution)/shard_map/ppermute | solution.py:21
  319.0 33.1 %collective-permute-start.1 = (bf16[384,768]{1,0:T(8,128)(2,1)S(1)}, bf16[384,768]{1,0:T(8,128)(2,1)}, u32[]{:S(2)}, u32[]{:S(2)}) collective-permute-start(bf16[384,768]{1,0:T(8,128)(2,1)S(1)} %bitcast.95), channel_id=1, source_target_pairs={{0,7},{1,0},{2,1},{3,2},{4,3},{5,4},{6,5},{7,6},{8,15},{9,8},{10,9... | collective-permute-start | bytes 1769480 | tf_op jit(solution)/shard_map/ppermute | solution.py:26
  349.6 17.5 %collective-permute-start.2 = (bf16[384,768]{1,0:T(8,128)(2,1)S(1)}, bf16[384,768]{1,0:T(8,128)(2,1)}, u32[]{:S(2)}, u32[]{:S(2)}) collective-permute-start(bf16[384,768]{1,0:T(8,128)(2,1)S(1)} %collective-permute-done), channel_id=1, source_target_pairs={{0,1},{1,2},{2,3},{3,4},{4,5},{5,6},{6,7},{7,0},{8,9},{9,10},{10,1... | collective-permute-start | bytes 1769480 | tf_op jit(solution)/shard_map/ppermute | solution.py:21
  352.1 28.8 %collective-permute-start.3 = (bf16[384,768]{1,0:T(8,128)(2,1)}, bf16[384,768]{1,0:T(8,128)(2,1)}, u32[]{:S(2)}, u32[]{:S(2)}) collective-permute-start(bf16[384,768]{1,0:T(8,128)(2,1)} %collective-permute-done.1), channel_id=1, source_target_pairs={{0,7},{1,0},{2,1},{3,2},{4,3},{5,4},{6,5},{7,6},{8,15},{9,8},{10,9... | collective-permute-start | bytes 1769480 | tf_op jit(solution)/shard_map/ppermute | solution.py:26
  367.1 33.5 %collective-permute-start.4 = (bf16[384,768]{1,0:T(8,128)(2,1)}, bf16[384,768]{1,0:T(8,128)(2,1)}, u32[]{:S(2)}, u32[]{:S(2)}) collective-permute-start(bf16[384,768]{1,0:T(8,128)(2,1)} %collective-permute-done.2), channel_id=1, source_target_pairs={{0,1},{1,2},{2,3},{3,4},{4,5},{5,6},{6,7},{7,0},{8,9},{9,10},{10,1... | collective-permute-start | bytes 1769480 | tf_op jit(solution)/shard_map/ppermute | solution.py:21
  369.4 17.6 %copy-start.24 = (bf16[384,768]{1,0:T(8,128)(2,1)S(1)}, bf16[384,768]{1,0:T(8,128)(2,1)}, u32[]{:S(2)}) copy-start(bf16[384,768]{1,0:T(8,128)(2,1)} %copy-done.23) | copy-start | bytes 1769476
  380.9 43.3 %collective-permute-start.5 = (bf16[384,768]{1,0:T(8,128)(2,1)}, bf16[384,768]{1,0:T(8,128)(2,1)S(1)}, u32[]{:S(2)}, u32[]{:S(2)}) collective-permute-start(bf16[384,768]{1,0:T(8,128)(2,1)} %collective-permute-done.3), channel_id=1, source_target_pairs={{0,7},{1,0},{2,1},{3,2},{4,3},{5,4},{6,5},{7,6},{8,15},{9,8},{10,9... | collective-permute-start | bytes 1769480 | tf_op jit(solution)/shard_map/ppermute | solution.py:26
  400.6 28.0 %collective-permute-start.6 = (bf16[384,768]{1,0:T(8,128)(2,1)}, bf16[384,768]{1,0:T(8,128)(2,1)S(1)}, u32[]{:S(2)}, u32[]{:S(2)}) collective-permute-start(bf16[384,768]{1,0:T(8,128)(2,1)} %collective-permute-done.4), channel_id=1, source_target_pairs={{0,1},{1,2},{2,3},{3,4},{4,5},{5,6},{6,7},{7,0},{8,9},{9,10},{10,1... | collective-permute-start | bytes 1769480 | tf_op jit(solution)/shard_map/ppermute | solution.py:21
  402.9 25.9 %copy-start.15 = (bf16[12,64,128]{2,1,0:T(8,128)(2,1)S(1)}, bf16[12,64,128]{2,1,0:T(8,128)(2,1)}, u32[]{:S(2)}) copy-start(bf16[12,64,128]{2,1,0:T(8,128)(2,1)} %copy-done.14) | copy-start | bytes 589828
  402.9 25.9 %copy-start.17 = (bf16[12,64,128]{2,1,0:T(8,128)(2,1)S(1)}, bf16[12,64,128]{2,1,0:T(8,128)(2,1)}, u32[]{:S(2)}) copy-start(bf16[12,64,128]{2,1,0:T(8,128)(2,1)} %copy-done.16) | copy-start | bytes 589828
  404.1 25.0 %copy-start.3 = (bf16[1,768,2304]{2,1,0:T(8,128)(2,1)S(1)}, bf16[1,768,2304]{2,1,0:T(8,128)(2,1)}, u32[]{:S(2)}) copy-start(bf16[1,768,2304]{2,1,0:T(8,128)(2,1)} %all-gather.17.cloned.1.call-done) | copy-start | bytes 10616836
  405.3 23.7 %copy-start.38 = (f32[128]{0:T(128)S(1)}, f32[128]{0:T(128)}, u32[]{:S(2)}) copy-start(f32[128]{0:T(128)} %copy-done.36) | copy-start | bytes 1540
  405.3 23.7 %copy-start.43 = (f32[128]{0:T(128)S(1)}, f32[128]{0:T(128)}, u32[]{:S(2)}) copy-start(f32[128]{0:T(128)} %copy-done.41) | copy-start | bytes 1540
  (39 other events, 94.2 us)
Sparse Core Ops, SparseCore 0:
  10.3 68.5 all-gather.16
  81.1 39.6 all-gather.18
  123.0 78.6 all-gather.20
  203.7 78.0 all-gather.22
  292.6 103.3 reduce-scatter.6
  399.6 140.0 reduce-scatter.4
  543.7 162.3 reduce-scatter.8
  710.1 162.4 reduce-scatter.10
  875.3 74.4 all-reduce.20
